TPU v7x, 32 devices: a whole 2x2x4 slice. The times are simulated.
32 devices in a mesh: grp: 4 (over z), seq: 8 (over y, x, core).
Axes of the slice: x: 2, y: 2, z: 4, core: 2. Of those that a mesh axis runs over, the one named last changes fastest.
Arguments:
- tokens: bfloat16 [4096, 2048], P(('grp', 'seq')), may hold values from -6 to 6
- norm_gains: float32 [2, 2048], replicated, may hold values from 0.5 to 1.5
- norm_biases: float32 [2, 2048], replicated, may hold values from -1 to 1
- mix_weight: bfloat16 [2048, 3, 2048], P(None, None, 'seq'), may hold values from -0.125 to 0.125
- mix_bias: bfloat16 [3, 2048], P(None, 'seq'), may hold values from -1.796875 to 1.796875
- out_weight: bfloat16 [2048, 2048], P('seq'), may hold values from -0.5 to 0.5
- gate_up_weight: bfloat16 [2048, 2, 5632], P(None, None, 'seq'), may hold values from -0.125 to 0.125
- down_weight: bfloat16 [5632, 2048], P('seq'), may hold values from -0.078125 to 0.078125
- row_lengths: int32 [8], replicated, may hold values from 128 to 1024, as said below
- row_group: int32 [8], replicated, may hold values from 0 to 3, as said below
- cotangent: bfloat16 [4096, 2048], P(('grp', 'seq')), may hold values from -6 to 6
Outputs:
- layer_out: bfloat16 [4096, 2048], P(('grp', 'seq'))
- tokens_grad: bfloat16 [4096, 2048], P(('grp', 'seq'))
- gains_grad: float32 [2, 2048], replicated
- biases_grad: float32 [2, 2048], replicated
- mix_grad: float32 [2048, 3, 2048], P(None, None, 'seq')
- mix_bias_grad: float32 [3, 2048], P(None, 'seq')
- out_grad: float32 [2048, 2048], P('seq')
- gate_up_grad: float32 [2048, 2, 5632], P(None, None, 'seq')
- down_grad: float32 [5632, 2048], P('seq')
Inputs may be any that keep to these rules, and one draw needn't show every extreme that they name: `row_lengths`: rows 0 to 1 are 1024 long; every other row's length is a multiple of 128 and at most 256. `row_group`: each of rows 0 to 1 fills a group alone; every other group holds exactly three of the other rows.
All inputs are finite; a program needn't handle non-finite values.
Results may differ from a plain program's by a relative error of at most 0.02.
Values may be sent and summed in bfloat16 or wider, within the bound.
A program may use at most 320 MiB of HBM per device.

v0:
```python
import math
import jax
import jax.numpy as jnp
from jax import lax
from jax.sharding import PartitionSpec as P

HEAD_DIM = 64
ROT = 16
EPS = 1e-05
NEG = -1e30
BASE = 10000.0


def layer_norm(values, gain, bias):
    centered = values - jnp.mean(values, axis=-1, keepdims=True)
    scale = lax.rsqrt(jnp.mean(centered * centered, axis=-1, keepdims=True) + EPS)
    unit = centered * scale
    return (unit * gain + bias, unit, scale)


def norm_back(incoming, unit, scale, gain):
    along = incoming * gain
    inner = jnp.mean(along, axis=-1, keepdims=True)
    cross = jnp.mean(along * unit, axis=-1, keepdims=True)
    return (
        scale * (along - inner - unit * cross),
        jnp.sum(incoming * unit, axis=0),
        jnp.sum(incoming, axis=0),
    )


def rotate(values, where, sign):
    half = ROT // 2
    freq = BASE ** (-jnp.arange(half, dtype=jnp.float32) / half)
    angle = where.astype(jnp.float32)[:, None] * freq[None, :]
    cosine = jnp.cos(angle)[:, None, :]
    sine = sign * jnp.sin(angle)[:, None, :]
    first = values[..., :half]
    second = values[..., half:ROT]
    return jnp.concatenate(
        [first * cosine - second * sine, second * cosine + first * sine, values[..., ROT:]], axis=-1
    )


def unrotate(lowered, where):
    wide = lowered.astype(jnp.float32)
    turned = jnp.stack(
        [rotate(wide[:, 0], where, -1.0), rotate(wide[:, 1], where, -1.0), wide[:, 2]], axis=1
    )
    return turned.reshape(lowered.shape[0], 3, -1).astype(jnp.bfloat16)


def slot_rows(row_lengths, row_group, group, slots):
    order = jnp.arange(row_lengths.shape[0], dtype=jnp.int32)
    same = row_group == group
    earlier = (order[:, None] > order[None, :]) & same[None, :]
    begin = jnp.sum(jnp.where(earlier, row_lengths[None, :], 0), axis=1)
    finish = begin + row_lengths
    inside = same[None, :] & (slots[:, None] >= begin[None, :]) & (slots[:, None] < finish[None, :])
    label = jnp.sum(jnp.where(inside, order[None, :] + 1, 0), axis=1) - 1
    offset = jnp.sum(jnp.where(inside, slots[:, None] - begin[None, :], 0), axis=1)
    load = jnp.sum(jnp.where(same, row_lengths, 0))
    return (label, jnp.where(label < 0, slots - load, offset))


def block_scores(query, key, label, start, block):
    part = lax.dynamic_slice_in_dim(query, start, block, 0)
    rows = start + jnp.arange(block, dtype=jnp.int32)
    columns = jnp.arange(label.shape[0], dtype=jnp.int32)
    label_rows = lax.dynamic_slice_in_dim(label, start, block, 0)
    allowed = (label_rows[:, None] == label[None, :]) & (rows[:, None] >= columns[None, :])
    scores = jnp.einsum("qhe,khe->hqk", part, key, preferred_element_type=jnp.float32) * (
        1.0 / math.sqrt(query.shape[-1])
    )
    return (part, jnp.where(allowed[None], scores, NEG))


def attend(query, key, value, label, block):

    def one_block(index):
        part, scores = block_scores(query, key, label, index * block, block)
        top = jnp.max(scores, axis=-1, keepdims=True)
        weights = jnp.exp(scores - top)
        totals = jnp.sum(weights, axis=-1, keepdims=True)
        probs = (weights / totals).astype(jnp.bfloat16)
        mixed = jnp.einsum("hqk,khe->qhe", probs, value, preferred_element_type=jnp.float32)
        return (mixed, top[..., 0] + jnp.log(totals[..., 0]))

    mixed, log_totals = lax.map(one_block, jnp.arange(query.shape[0] // block, dtype=jnp.int32))
    return (mixed.reshape(query.shape), log_totals)


def attend_back(query, key, value, label, log_totals, mixed_back, block):
    scale = 1.0 / math.sqrt(query.shape[-1])

    def one_block(carry, index):
        key_back, value_back = carry
        start = index * block
        part, scores = block_scores(query, key, label, start, block)
        back_part = lax.dynamic_slice_in_dim(mixed_back, start, block, 0)
        probs = jnp.exp(scores - log_totals[index][..., None])
        value_back = value_back + jnp.einsum(
            "hqk,qhe->khe",
            probs.astype(jnp.bfloat16),
            back_part,
            preferred_element_type=jnp.float32,
        )
        probs_back = jnp.einsum(
            "qhe,khe->hqk", back_part, value, preferred_element_type=jnp.float32
        )
        inner = jnp.sum(probs_back * probs, axis=-1, keepdims=True)
        score_back = (probs * (probs_back - inner)).astype(jnp.bfloat16)
        query_back = (
            jnp.einsum("hqk,khe->qhe", score_back, key, preferred_element_type=jnp.float32) * scale
        )
        key_back = (
            key_back
            + jnp.einsum("hqk,qhe->khe", score_back, part, preferred_element_type=jnp.float32)
            * scale
        )
        return ((key_back, value_back), query_back)

    empty = jnp.zeros(key.shape, jnp.float32)
    (key_back, value_back), query_back = lax.scan(
        one_block, (empty, empty), jnp.arange(query.shape[0] // block, dtype=jnp.int32)
    )
    return (query_back.reshape(query.shape), key_back, value_back)


def silu_parts(gate_up):
    gate = gate_up[:, 0]
    upper = gate_up[:, 1]
    sigma = jax.nn.sigmoid(gate)
    return (gate * sigma * upper, gate, upper, sigma)


def gate_back(hidden_back, gate, upper, sigma):
    gate_part = hidden_back * upper * sigma * (1.0 + gate * (1.0 - sigma))
    up_part = hidden_back * gate * sigma
    return jnp.stack([gate_part, up_part], axis=1).astype(jnp.bfloat16)


def gather_rows(values):
    return lax.all_gather(values, "seq", axis=0, tiled=True)


def summed_rows(product, left):
    return lax.psum_scatter(
        product(left).astype(jnp.bfloat16), "seq", scatter_dimension=0, tiled=True
    ).astype(jnp.float32)


def on_device(
    tokens,
    norm_gains,
    norm_biases,
    mix_weight,
    mix_bias,
    out_weight,
    gate_up_weight,
    down_weight,
    row_lengths,
    row_group,
    cotangent,
):
    seq_count = lax.axis_size("seq")
    shard = lax.axis_index("seq")
    group = lax.axis_index("grp")
    slots_dev = tokens.shape[0]
    width = tokens.shape[1]
    group_slots = slots_dev * seq_count
    block = min(512, group_slots)
    local_width = width // seq_count
    local_heads = local_width // HEAD_DIM
    mine = shard * slots_dev + jnp.arange(slots_dev, dtype=jnp.int32)
    label_mine, place_mine = slot_rows(row_lengths, row_group, group, mine)
    label_all, place_all = slot_rows(
        row_lengths, row_group, group, jnp.arange(group_slots, dtype=jnp.int32)
    )
    inputs = tokens.astype(jnp.float32)
    upstream = cotangent.astype(jnp.float32) * (label_mine >= 0).astype(jnp.float32)[:, None]
    upstream_low = upstream.astype(jnp.bfloat16)
    normed, unit_one, scale_one = layer_norm(inputs, norm_gains[0], norm_biases[0])
    normed_low = normed.astype(jnp.bfloat16)
    mix_full, bias_full, out_full = (
        lax.all_gather(mix_weight, "seq", axis=2, tiled=True),
        lax.all_gather(mix_bias, "seq", axis=1, tiled=True),
        lax.all_gather(out_weight, "seq", axis=0, tiled=True),
    )
    mixin = jnp.einsum(
        "td,dcf->tcf", normed_low, mix_full, preferred_element_type=jnp.float32
    ) + bias_full.astype(jnp.float32)
    heads_in = mixin.reshape(slots_dev, 3, width // HEAD_DIM, HEAD_DIM)
    sending = jnp.stack(
        [
            rotate(heads_in[:, 0], place_mine, 1.0),
            rotate(heads_in[:, 1], place_mine, 1.0),
            heads_in[:, 2],
        ],
        axis=1,
    ).astype(jnp.bfloat16)
    arrived = lax.all_to_all(
        sending.reshape(slots_dev, 3, seq_count, local_width),
        "seq",
        split_axis=2,
        concat_axis=0,
        tiled=True,
    )
    arrived = arrived.reshape(group_slots, 3, local_heads, HEAD_DIM)
    query, key, value = (arrived[:, 0], arrived[:, 1], arrived[:, 2])
    mixed, log_totals = attend(query, key, value, label_all, block)
    attended = lax.all_to_all(
        mixed.reshape(group_slots, local_width).astype(jnp.bfloat16),
        "seq",
        split_axis=0,
        concat_axis=1,
        tiled=True,
    )
    resid = inputs + jnp.dot(attended, out_full, preferred_element_type=jnp.float32)
    normed_two, unit_two, scale_two = layer_norm(resid, norm_gains[1], norm_biases[1])
    normed_two_all = gather_rows(normed_two.astype(jnp.bfloat16))
    gate_up = jnp.einsum(
        "td,dcf->tcf", normed_two_all, gate_up_weight, preferred_element_type=jnp.float32
    )
    hidden, gate, upper, sigma = silu_parts(gate_up)
    hidden_low = hidden.astype(jnp.bfloat16)

    def down_product(part):
        return jnp.dot(part, down_weight, preferred_element_type=jnp.float32)

    layer_out = resid + summed_rows(down_product, hidden_low)
    upstream_all = gather_rows(upstream_low)
    down_shard = jnp.einsum(
        "tf,td->fd", hidden_low, upstream_all, preferred_element_type=jnp.float32
    )
    hidden_back = jnp.einsum(
        "td,fd->tf", upstream_all, down_weight, preferred_element_type=jnp.float32
    )
    gate_up_back = gate_back(hidden_back, gate, upper, sigma)
    gate_up_shard = jnp.einsum(
        "td,tcf->dcf", normed_two_all, gate_up_back, preferred_element_type=jnp.float32
    )

    def gate_up_product(part):
        return jnp.einsum("tcf,dcf->td", part, gate_up_weight, preferred_element_type=jnp.float32)

    normed_two_back = summed_rows(gate_up_product, gate_up_back)
    resid_part, gain_two, bias_two = norm_back(normed_two_back, unit_two, scale_two, norm_gains[1])
    resid_back = upstream + resid_part
    branch_low = resid_back.astype(jnp.bfloat16)
    out_term = jnp.einsum("te,td->ed", attended, branch_low, preferred_element_type=jnp.float32)
    attended_back = jnp.einsum(
        "td,ed->te", branch_low, out_full, preferred_element_type=jnp.float32
    ).astype(jnp.bfloat16)
    heads_back = lax.all_to_all(
        attended_back, "seq", split_axis=1, concat_axis=0, tiled=True
    ).reshape(group_slots, local_heads, HEAD_DIM)
    query_back, key_back, value_back = attend_back(
        query, key, value, label_all, log_totals, heads_back, block
    )
    lowered = (
        jnp.stack([query_back, key_back, value_back], axis=1)
        .astype(jnp.bfloat16)
        .reshape(group_slots, 3, 1, local_width)
    )
    returned = lax.all_to_all(lowered, "seq", split_axis=0, concat_axis=2, tiled=True).reshape(
        slots_dev, 3, width // HEAD_DIM, HEAD_DIM
    )
    mixin_back = unrotate(returned, place_mine)
    mix_term = jnp.einsum("td,tcf->dcf", normed_low, mixin_back, preferred_element_type=jnp.float32)
    bias_term = jnp.sum(mixin_back, axis=0, dtype=jnp.float32)
    normed_back = jnp.einsum(
        "tcf,dcf->td", mixin_back, mix_full, preferred_element_type=jnp.float32
    )
    mix_shard, bias_shard, out_shard = (
        lax.psum_scatter(
            mix_term.astype(jnp.bfloat16), "seq", scatter_dimension=2, tiled=True
        ).astype(jnp.float32),
        lax.psum_scatter(
            bias_term.astype(jnp.bfloat16), "seq", scatter_dimension=1, tiled=True
        ).astype(jnp.float32),
        lax.psum_scatter(
            out_term.astype(jnp.bfloat16), "seq", scatter_dimension=0, tiled=True
        ).astype(jnp.float32),
    )
    tokens_part, gain_one, bias_one = norm_back(normed_back, unit_one, scale_one, norm_gains[0])
    tokens_grad = (resid_back + tokens_part).astype(jnp.bfloat16)
    mix_grad, mix_bias_grad, out_grad, gate_up_grad, down_grad = (
        lax.psum(mix_shard.astype(jnp.bfloat16), "grp").astype(jnp.float32),
        lax.psum(bias_shard.astype(jnp.bfloat16), "grp").astype(jnp.float32),
        lax.psum(out_shard.astype(jnp.bfloat16), "grp").astype(jnp.float32),
        lax.psum(gate_up_shard.astype(jnp.bfloat16), "grp").astype(jnp.float32),
        lax.psum(down_shard.astype(jnp.bfloat16), "grp").astype(jnp.float32),
    )
    gains_grad, biases_grad = lax.psum(
        (jnp.stack([gain_one, gain_two]), jnp.stack([bias_one, bias_two])), ("grp", "seq")
    )
    return (
        layer_out.astype(jnp.bfloat16),
        tokens_grad,
        gains_grad,
        biases_grad,
        mix_grad,
        mix_bias_grad,
        out_grad,
        gate_up_grad,
        down_grad,
    )


def solution(mesh):
    placed = (
        P(("grp", "seq"), None),
        P(),
        P(),
        P(None, None, "seq"),
        P(None, "seq"),
        P("seq", None),
        P(None, None, "seq"),
        P("seq", None),
        P(),
        P(),
        P(("grp", "seq"), None),
    )
    return jax.shard_map(
        on_device,
        mesh=mesh,
        in_specs=placed,
        out_specs=(
            P(("grp", "seq"), None),
            P(("grp", "seq"), None),
            P(),
            P(),
            P(None, None, "seq"),
            P(None, "seq"),
            P("seq", None),
            P(None, None, "seq"),
            P("seq", None),
        ),
        check_vma=False,
    )
```

profile of v0, /device:TPU:0, one launch (start us, length us, event | category | flops | bytes accessed | tf_op | source)
XLA Modules:
  0.0 1248.3 jit_solution(738130817734868844)
XLA Ops:
  9.5 10.4 all_gather.16
  21.9 121.0 %all-gather.5.cloned.1.call-done = bf16[2048,3,2048]{2,0,1:T(8,128)(2,1)} async-done(((bf16[2048,3,256]{2,0,1:T(8,128)(2,1)}), bf16[2048,3,2048]{2,0,1:T(8,128)(2,1)}) %all-gather.5.cloned.1.call-update) | async-done | bytes 25165840 | tf_op jit(solution)/shard_map/all_gather | solution.py:186
  143.0 13.4 %convolution_add_fusion = f32[128,3,2048]{2,0,1:T(8,128)} fusion(bf16[2048,3,2048]{2,0,1:T(8,128)(2,1)} %all-gather.5.cloned.1.call-done, f32[3,2048]{1,0:T(4,128)S(1)} %convert_element_type.139, bf16[128,2048]{1,0:T(8,128)(2,1)S(1)} %copy-done.5, f32[2048]{0:T(1024)S(1)} %bitcast.195, f32[2048]{0:T(1024)S(1)} %bitcast.191, f32[128]{0:T(128)S(1)} %add_rsqrt_fusion.1, ...), kind=kOutput, calls=%fused_computation.63 | convolution fusion | flops 3223584768 | bytes 28877824 | tf_op jit(solution)/shard_map/td,dcf->tcf/dot_general | solution.py:190
  156.4 3.5 copy.90
  164.7 4.5 all-to-all-start
  169.3 35.6 %all-to-all-done = bf16[128,3,8,256]{0,3,1,2:T(8,128)(2,1)} async-done(((bf16[128,3,8,256]{0,3,1,2:T(8,128)(2,1)}), bf16[128,3,8,256]{0,3,1,2:T(8,128)(2,1)}, u32[]{:S(2)}, u32[]{:S(2)}) %all-to-all-start) | async-done | bytes 1572896 | tf_op jit(solution)/shard_map/all_to_all | solution.py:202
  204.9 3.6 copy.92
  208.5 3.7 reshape.381
  212.2 2.6 slice_bitcast_fusion.6
  215.6 21.5 %while.27 = (s32[]{:T(128)}, bf16[2,512,4,64]{1,3,2,0:T(8,128)(2,1)}, f32[2,4,512]{2,1,0:T(4,128)S(1)}, s32[2]{0:T(128)S(1)}, s32[1024]{0:T(1024)S(1)}, /*index=...) while((s32[]{:T(128)}, ...), condition=%wide.region_10.11_spmd, body=%wide.region_7.10_spmd.sunk | while | flops 563608064 | bytes 35469596 | solution.py:89
  217.5 2.6 fusion.126
  222.5 3.0 fusion.128
  228.2 2.6 fusion.126
  233.3 3.0 fusion.128
  243.5 4.2 all-to-all-start.1
  247.8 9.7 all-to-all-done.1
  257.4 4.9 fusion.81
  266.9 33.4 %all-gather.9.cloned.1.call-done = bf16[1024,2048]{1,0:T(8,128)(2,1)} async-done(((bf16[128,2048]{1,0:T(8,128)(2,1)}), bf16[1024,2048]{1,0:T(8,128)(2,1)}) %all-gather.9.cloned.1.call-update) | async-done | bytes 4194320 | tf_op jit(solution)/shard_map/all_gather | solution.py:144
  300.4 11.0 fusion.39
  311.4 28.1 %all-gather.11.cloned.1.call-done = bf16[1024,2048]{1,0:T(8,128)(2,1)} async-done(((bf16[128,2048]{1,0:T(8,128)(2,1)}), bf16[1024,2048]{1,0:T(8,128)(2,1)}) %all-gather.11.cloned.1.call-update) | async-done | bytes 4194320 | tf_op jit(solution)/shard_map/all_gather | solution.py:144
  339.5 8.3 fusion.45
  349.4 11.0 bitcast_convert_fusion
  360.4 6.4 convolution_convert_fusion.3
  366.9 45.0 %reduce-scatter.10.cloned.1.call-done = bf16[128,2048]{1,0:T(8,128)(2,1)} async-done(((bf16[1024,2048]{1,0:T(8,128)(2,1)}), bf16[128,2048]{1,0:T(8,128)(2,1)}) %reduce-scatter.10.cloned.1.call-update) | async-done | bytes 524304 | tf_op jit(solution)/shard_map/reduce_scatter | solution.py:148
  414.0 53.4 %reduce-scatter.8.cloned.1.call-done = bf16[128,2048]{1,0:T(8,128)(2,1)} async-done(((bf16[1024,2048]{1,0:T(8,128)(2,1)}), bf16[128,2048]{1,0:T(8,128)(2,1)}) %reduce-scatter.8.cloned.1.call-update) | async-done | bytes 524304 | tf_op jit(solution)/shard_map/reduce_scatter | solution.py:148
  469.7 7.1 convolution_convert_fusion.1
  476.8 6.3 convolution_convert_fusion.5
  484.0 3.5 all-to-all-start.2
  487.7 9.4 all-to-all-done.2
  501.1 31.6 %while.28 = (s32[]{:T(128)}, f32[1024,4,64]{0,2,1:T(8,128)S(1)}, f32[1024,4,64]{0,2,1:T(8,128)}, bf16[2,512,4,64]{1,3,2,0:T(8,128)(2,1)}, s32[2]{0:T(128)S(1)}, ...) while((s32[]{:T(128)}, f32[1024,4,64]{0,2,1:T(8,128)S(1)}, ...), condition=%wide.region_19.20_spmd.clone, body=%wide.region_17.19_spmd.clone.sunk | while | flops 1376647680 | bytes 87103920 | solution.py:124
  506.4 2.5 fusion.141
  508.9 3.2 multiply_reduce_fusion.4
  522.2 2.6 fusion.141
  524.7 3.2 multiply_reduce_fusion.4
  537.6 3.0 copy.98
  540.5 29.5 %all_to_all.56 = bf16[1024,3,1,256]{3,1,2,0:T(4,128)(2,1)S(1)} all-to-all(bf16[1024,3,1,256]{3,1,2,0:T(4,128)(2,1)S(1)} %copy.98), channel_id=1, replica_groups=mesh['grp'=4,'seq'=8] {'seq'}, dimensions={0} | all-to-all | bytes 3145728 | tf_op jit(solution)/shard_map/all_to_all | solution.py:266
  578.5 12.0 convolution_convert_fusion
  590.6 10.8 convolution_convert_fusion.2
  603.1 8.9 convolution_convert_fusion.4
  612.0 134.7 %reduce-scatter.12.cloned.1.call-done = bf16[2048,3,256]{2,0,1:T(8,128)(2,1)} async-done(((bf16[2048,3,2048]{2,0,1:T(8,128)(2,1)}), bf16[2048,3,256]{2,0,1:T(8,128)(2,1)}) %reduce-scatter.12.cloned.1.call-update) | async-done | bytes 3145744 | tf_op jit(solution)/shard_map/reduce_scatter | solution.py:276
  746.7 14.6 %fusion.59 = (f32[2048]{0:T(1024)S(1)}, f32[128]{0:T(128)S(1)}, f32[128]{0:T(128)S(1)}, f32[2048]{0:T(1024)S(1)}, f32[128,2048]{1,0:T(8,128)}) fusion(bf16[128,2048]{1,0:T(8,128)(2,1)S(1)} %copy-done.6, f32[128]{0:T(128)S(1)} %copy-done.35, f32[128]{0:T(128)S(1)} %copy-done.33, f32[2048]{0:T(1024)S(1)} %bitcast.193, ...), kind=kOutput, calls=%fused_computation.93 | convolution fusion | flops 3225415680 | bytes 28338176 | tf_op jit(solution)/shard_map/tcf,dcf->td/dot_general | solution.py:272
  761.4 40.2 %all-reduce = (f32[2,2048]{1,0:T(2,128)}, f32[2,2048]{1,0:T(2,128)}) all-reduce(f32[2,2048]{1,0:T(2,128)S(1)} %pad_maximum_fusion.10, f32[2,2048]{1,0:T(2,128)S(1)} %pad_maximum_fusion.11), channel_id=1, replica_groups=mesh['grp'=4,'seq'=8] {'grp','seq'}, use_global_device_ids=true, to_apply=%region_24.25 | all-reduce | flops 8192 | bytes 65536 | tf_op jit(solution)/shard_map/psum | solution.py:295
  805.0 12.3 psum.52
  817.9 407.1 %all-reduce.4.cloned.1.call-done = (bf16[2048,3,256]{2,0,1:T(8,128)(2,1)}, bf16[256,2048]{1,0:T(8,128)(2,1)}, bf16[2048,2,704]{0,2,1:T(8,128)(2,1)}, bf16[704,2048]{1,0:T(8,128)(2,1)}) async-done(((bf16[2048,3,256]{2,0,1:T(8,128)(2,1)}, bf16[256,2048]{1,0:T(8,128)(2,1)}, bf16[2048,2,704]{0,2,1:T(8,128)(2,1)}, bf16[704,2048]{1,0:T(8,128)(2,1)}), (bf16[2048,3,256]{2,0,1:T(8,128)(2,1)}, ...) | async-done | bytes 12845072 | tf_op jit(solution)/shard_map/psum | solution.py:289
  1225.0 2.9 convert_element_type.164
  1228.0 3.7 convert_element_type.161
  1231.7 3.3 convert_element_type.168
  1235.0 6.0 convert_element_type.166
  (232 shorter events, 74.7 us)
Async XLA Ops:
  7.2 332.3 %copy-start = (bf16[704,2048]{1,0:T(8,128)(2,1)S(1)}, bf16[704,2048]{1,0:T(8,128)(2,1)}, u32[]{:S(2)}) copy-start(bf16[704,2048]{1,0:T(8,128)(2,1)} %param.22) | copy-start | bytes 8650756
  7.2 1.6 copy-start.38
  7.2 2.3 copy-start.36
  7.2 12.8 %copy-start.5 = (bf16[128,2048]{1,0:T(8,128)(2,1)S(1)}, bf16[128,2048]{1,0:T(8,128)(2,1)}, u32[]{:S(2)}) copy-start(bf16[128,2048]{1,0:T(8,128)(2,1)} %param.15) | copy-start | bytes 1572868
  7.2 14.6 %copy-start.30 = (f32[2,2048]{1,0:T(2,128)S(1)}, f32[2,2048]{1,0:T(2,128)}, u32[]{:S(2)}) copy-start(f32[2,2048]{1,0:T(2,128)} %param.16) | copy-start | bytes 49156
  7.2 14.6 %copy-start.31 = (f32[2,2048]{1,0:T(2,128)S(1)}, f32[2,2048]{1,0:T(2,128)}, u32[]{:S(2)}) copy-start(f32[2,2048]{1,0:T(2,128)} %param.17) | copy-start | bytes 49156
  7.3 135.7 %all-gather.5.cloned.1.call-start = ((), (), s32[]{:S(2)}) async-start(), calls=%async_computation.9 | async-start | bytes 28311552 | tf_op jit(solution)/shard_map/all_gather | solution.py:186
  8.0 239.8 %all-gather.7.cloned.1.call-start = ((), (), s32[]{:S(2)}) async-start(), calls=%async_computation.10 | async-start | bytes 9437184 | tf_op jit(solution)/shard_map/all_gather | solution.py:188
  20.2 136.2 %copy-start.32 = (f32[128]{0:T(128)}, f32[128]{0:T(128)S(1)}, u32[]{:S(2)}) copy-start(f32[128]{0:T(128)S(1)} %broadcast_multiply_fusion.6) | copy-start | bytes 1540
  20.5 135.9 %copy-start.34 = (f32[128]{0:T(128)}, f32[128]{0:T(128)S(1)}, u32[]{:S(2)}) copy-start(f32[128]{0:T(128)S(1)} %add_rsqrt_fusion.1) | copy-start | bytes 1540
  21.9 141.2 %copy-start.25 = (f32[128,8]{0,1:T(8,128)}, f32[128,8]{0,1:T(8,128)S(1)}, u32[]{:S(2)}) copy-start(f32[128,8]{0,1:T(8,128)S(1)} %get-tuple-element.253) | copy-start | bytes 12292
  21.9 134.5 %copy-start.21 = (f32[1,2048]{1,0:T(1,128)}, f32[1,2048]{1,0:T(1,128)S(1)}, u32[]{:S(2)}) copy-start(f32[1,2048]{1,0:T(1,128)S(1)} %get-tuple-element.244) | copy-start | bytes 24580
  21.9 134.4 %copy-start.23 = (f32[1,2048]{1,0:T(1,128)}, f32[1,2048]{1,0:T(1,128)S(1)}, u32[]{:S(2)}) copy-start(f32[1,2048]{1,0:T(1,128)S(1)} %get-tuple-element.246) | copy-start | bytes 24580
  164.7 40.2 %all-to-all-start = ((bf16[128,3,8,256]{0,3,1,2:T(8,128)(2,1)}), bf16[128,3,8,256]{0,3,1,2:T(8,128)(2,1)}, u32[]{:S(2)}, u32[]{:S(2)}) async-start(bf16[128,3,8,256]{0,3,1,2:T(8,128)(2,1)} %copy.91), calls=%async_computation | async-start | bytes 3145728 | tf_op jit(solution)/shard_map/all_to_all | solution.py:202
  220.1 2.4 copy-start.7
  220.1 2.4 copy-start.16
  230.9 2.4 copy-start.7
  230.9 2.4 copy-start.16
  243.5 13.9 %all-to-all-start.1 = ((bf16[8,128,256]{1,2,0:T(8,128)(2,1)}), bf16[8,128,256]{1,2,0:T(8,128)(2,1)}, u32[]{:S(2)}, u32[]{:S(2)}) async-start(bf16[8,128,256]{1,2,0:T(8,128)(2,1)} %copy.94), calls=%async_computation.1 | async-start | bytes 1048576 | tf_op jit(solution)/shard_map/all_to_all | solution.py:212
  247.7 52.7 %all-gather.9.cloned.1.call-start = ((), (), s32[]{:S(2)}) async-start(), calls=%async_computation.11 | async-start | bytes 4718592 | tf_op jit(solution)/shard_map/all_gather | solution.py:144
  264.4 75.0 %all-gather.11.cloned.1.call-start = ((), (), s32[]{:S(2)}) async-start(), calls=%async_computation.13 | async-start | bytes 4718592 | tf_op jit(solution)/shard_map/all_gather | solution.py:144
  266.5 145.4 %reduce-scatter.10.cloned.1.call-start = ((), (), s32[]{:S(2)}) async-start(), calls=%async_computation.14 | async-start | bytes 4718592 | tf_op jit(solution)/shard_map/reduce_scatter | solution.py:148
  347.8 1.6 copy-start.40
  360.4 107.0 %reduce-scatter.8.cloned.1.call-start = ((), (), s32[]{:S(2)}) async-start(), calls=%async_computation.12 | async-start | bytes 4718592 | tf_op jit(solution)/shard_map/reduce_scatter | solution.py:148
  366.8 45.0 %copy-start.4 = (f32[128,2048]{1,0:T(8,128)S(1)}, f32[128,2048]{1,0:T(8,128)}, u32[]{:S(2)}) copy-start(f32[128,2048]{1,0:T(8,128)} %copy-done.3) | copy-start | bytes 3145732
  366.8 100.5 %copy-start.18 = (bf16[128,2048]{1,0:T(8,128)(2,1)S(1)}, bf16[128,2048]{1,0:T(8,128)(2,1)}, u32[]{:S(2)}) copy-start(bf16[128,2048]{1,0:T(8,128)(2,1)} %param.25) | copy-start | bytes 1572868
  366.9 245.1 %reduce-scatter.14.cloned.1.call-start = ((), (), s32[]{:S(2)}) async-start(), calls=%async_computation.16 | async-start | bytes 9437184 | tf_op jit(solution)/shard_map/reduce_scatter | solution.py:282
  469.7 7.2 copy-start.9
  483.1 18.0 %copy-start.2 = (bf16[1024,4,64]{0,2,1:T(8,128)(2,1)S(1)}, bf16[1024,4,64]{0,2,1:T(8,128)(2,1)}, u32[]{:S(2)}) copy-start(bf16[1024,4,64]{0,2,1:T(8,128)(2,1)} %get-tuple-element.490) | copy-start | bytes 1572868
  483.1 18.0 %copy-start.8 = (bf16[1024,4,64]{0,2,1:T(8,128)(2,1)S(1)}, bf16[1024,4,64]{0,2,1:T(8,128)(2,1)}, u32[]{:S(2)}) copy-start(bf16[1024,4,64]{0,2,1:T(8,128)(2,1)} %get-tuple-element.491) | copy-start | bytes 1572868
  484.0 13.2 %all-to-all-start.2 = ((bf16[128,8,256]{2,0,1:T(8,128)(2,1)}), bf16[128,8,256]{2,0,1:T(8,128)(2,1)S(1)}, u32[]{:S(2)}, u32[]{:S(2)}) async-start(bf16[128,8,256]{2,0,1:T(8,128)(2,1)} %bitcast.142), calls=%async_computation.4 | async-start | bytes 1048576 | tf_op jit(solution)/shard_map/all_to_all | solution.py:255
  487.5 259.2 %reduce-scatter.12.cloned.1.call-start = ((), (), s32[]{:S(2)}) async-start(), calls=%async_computation.15 | async-start | bytes 28311552 | tf_op jit(solution)/shard_map/reduce_scatter | solution.py:276
  508.9 3.2 copy-start.20
  512.1 2.4 copy-start.14
  524.7 3.2 copy-start.20
  527.9 2.4 copy-start.14
  575.4 2.1 copy-start.26
  575.4 2.1 copy-start.29
  590.5 213.5 %reduce-scatter.16.cloned.1.call-start = ((), (), s32[]{:S(2)}) async-start(), calls=%async_computation.17 | async-start | bytes 589824
  602.8 622.3 %all-reduce.4.cloned.1.call-start = ((), (), s32[]{:S(2)}) async-start(), calls=%async_computation.18 | async-start | bytes 25690112 | tf_op jit(solution)/shard_map/psum | solution.py:289
  746.7 14.7 %copy-start.28 = (f32[2048]{0:T(1024)S(1)}, f32[2048]{0:T(1024)}, u32[]{:S(2)}) copy-start(f32[2048]{0:T(1024)} %get-tuple-element.165) | copy-start | bytes 24580
  746.7 14.7 %copy-start.27 = (f32[2048]{0:T(1024)S(1)}, f32[2048]{0:T(1024)}, u32[]{:S(2)}) copy-start(f32[2048]{0:T(1024)} %get-tuple-element.170) | copy-start | bytes 24580
  746.7 54.9 %copy-start.10 = (f32[128,2048]{1,0:T(8,128)S(1)}, f32[128,2048]{1,0:T(8,128)}, u32[]{:S(2)}) copy-start(f32[128,2048]{1,0:T(8,128)} %copy-done.9) | copy-start | bytes 3145732
  1225.0 2.9 copy-start.12
  1225.0 10.0 slice-start
  1228.0 3.7 copy-start.13
  1228.0 7.1 slice-start.1
  1235.0 6.0 copy-start.1
  (16 other events, 17.8 us)
Sparse Core Ops, SparseCore 0:
  10.0 132.9 all-gather.4
  144.9 68.7 all-gather.6
  264.5 35.7 all-gather.8
  302.7 36.7 all-gather.10
  360.5 51.3 reduce-scatter.9
  416.0 51.2 reduce-scatter.7
  476.9 71.4 reduce-scatter.13
  590.6 155.9 reduce-scatter.11
  750.0 34.2 reduce-scatter.15
  788.2 436.8 all-reduce.3
where the time goes:
time: 1250 us
  waiting for transfers between devices  879 us (70%)
  matrix products  145 us (12%)
  blocking collectives  92.4 us (7%)
  local copies, waits for them, and re-layouts  49.7 us (4%)
  other arithmetic  47.1 us (4%)
  between operations  15.2 us (1%)
  starting transfers between devices  13.4 us (1%)
    psum x1, waiting for transfers between devices, on_device(): lax.psum(mix_shard.astype(jnp.bfloat16), 'grp').astype(jnp.float32)  407 us
    reduce_scatter x1, waiting for transfers between devices, on_device(): lax.psum_scatter(mix_term.astype(jnp.bfloat16), 'seq', scatter_dimension=...  135 us
    all_gather x1, waiting for transfers between devices, on_device(): lax.all_gather(mix_weight, 'seq', axis=2, tiled=True)  121 us
    reduce_scatter x2, waiting for transfers between devices, summed_rows(): lax.psum_scatter(product(left).astype(jnp.bfloat16), 'seq', scatter_dimen...  98.3 us
    all_gather x2, waiting for transfers between devices, gather_rows(): return lax.all_gather(values, 'seq', axis=0, tiled=True)  61.5 us
    psum x1, blocking collectives, on_device(): lax.psum((jnp.stack([gain_one, gain_two]), jnp.stack([bias_one, bias_two]...  40.2 us
    all_to_all x1, waiting for transfers between devices, on_device(): lax.all_to_all(sending.reshape(slots_dev, 3, seq_count, local_width), 'se...  35.6 us
    all_to_all x1, blocking collectives, on_device(): lax.all_to_all(lowered, 'seq', split_axis=0, concat_axis=2, tiled=True)  29.5 us
  transfers between devices with their start and end apart: 13, of which 10 were waited for; matrix products, arithmetic and copies ran while one was open for 15% of the time, Pallas kernels for 0%

commit v1 on v0

--- a/solution.py
+++ b/solution.py
@@ -3,6 +3,7 @@
 import jax.numpy as jnp
 from jax import lax
 from jax.sharding import PartitionSpec as P
+from jax.lax import psum
 
 HEAD_DIM = 64
 ROT = 16
@@ -292,8 +293,8 @@
         lax.psum(gate_up_shard.astype(jnp.bfloat16), "grp").astype(jnp.float32),
         lax.psum(down_shard.astype(jnp.bfloat16), "grp").astype(jnp.float32),
     )
-    gains_grad, biases_grad = lax.psum(
-        (jnp.stack([gain_one, gain_two]), jnp.stack([bias_one, bias_two])), ("grp", "seq")
+    gains_grad, biases_grad = psum(
+        psum((jnp.stack([gain_one, gain_two]), jnp.stack([bias_one, bias_two])), "seq"), "grp"
     )
     return (
         layer_out.astype(jnp.bfloat16),

time: 1250 us -> 1250 us (level)
    psum x1 -> x2, blocking collectives: 40.2 us -> 43.3 us  [the longest x1 23.1 us: on_device(): psum((jnp.stack([gain_one, gain_two]), jnp.stack([bias_one, bias_two])),...]
where the time goes in v1:
time: 1250 us
  waiting for transfers between devices  877 us (70%)
  matrix products  145 us (12%)
  blocking collectives  94.3 us (8%)
  local copies, waits for them, and re-layouts  49.8 us (4%)
  other arithmetic  47.1 us (4%)
  between operations  15.2 us (1%)
  starting transfers between devices  13.4 us (1%)
    psum x1, waiting for transfers between devices, on_device(): lax.psum(mix_shard.astype(jnp.bfloat16), 'grp').astype(jnp.float32)  405 us
    reduce_scatter x1, waiting for transfers between devices, on_device(): lax.psum_scatter(mix_term.astype(jnp.bfloat16), 'seq', scatter_dimension=...  135 us
    all_gather x1, waiting for transfers between devices, on_device(): lax.all_gather(mix_weight, 'seq', axis=2, tiled=True)  121 us
    reduce_scatter x2, waiting for transfers between devices, summed_rows(): lax.psum_scatter(product(left).astype(jnp.bfloat16), 'seq', scatter_dimen...  98.3 us
    all_gather x2, waiting for transfers between devices, gather_rows(): return lax.all_gather(values, 'seq', axis=0, tiled=True)  61.5 us
    all_to_all x1, waiting for transfers between devices, on_device(): lax.all_to_all(sending.reshape(slots_dev, 3, seq_count, local_width), 'se...  35.6 us
    all_to_all x1, blocking collectives, on_device(): lax.all_to_all(lowered, 'seq', split_axis=0, concat_axis=2, tiled=True)  29.3 us
  transfers between devices with their start and end apart: 13, of which 10 were waited for; matrix products, arithmetic and copies ran while one was open for 15% of the time, Pallas kernels for 0%

profile of v1, /device:TPU:0, one launch (start us, length us, event | category | flops | bytes accessed | tf_op | source)
XLA Modules:
  0.0 1248.6 jit_solution(2970910060220202975)
XLA Ops:
  9.5 10.4 all_gather.16
  21.9 121.0 %all-gather.5.cloned.1.call-done = bf16[2048,3,2048]{2,0,1:T(8,128)(2,1)} async-done(((bf16[2048,3,256]{2,0,1:T(8,128)(2,1)}), bf16[2048,3,2048]{2,0,1:T(8,128)(2,1)}) %all-gather.5.cloned.1.call-update) | async-done | bytes 25165840 | tf_op jit(solution)/shard_map/all_gather | solution.py:187
  143.0 13.4 %convolution_add_fusion = f32[128,3,2048]{2,0,1:T(8,128)} fusion(bf16[2048,3,2048]{2,0,1:T(8,128)(2,1)} %all-gather.5.cloned.1.call-done, f32[3,2048]{1,0:T(4,128)S(1)} %convert_element_type.139, bf16[128,2048]{1,0:T(8,128)(2,1)S(1)} %copy-done.5, f32[2048]{0:T(1024)S(1)} %bitcast.195, f32[2048]{0:T(1024)S(1)} %bitcast.191, f32[128]{0:T(128)S(1)} %add_rsqrt_fusion.1, ...), kind=kOutput, calls=%fused_computation.63 | convolution fusion | flops 3223584768 | bytes 28877824 | tf_op jit(solution)/shard_map/td,dcf->tcf/dot_general | solution.py:191
  156.4 3.5 copy.90
  164.7 4.5 all-to-all-start
  169.3 35.6 %all-to-all-done = bf16[128,3,8,256]{0,3,1,2:T(8,128)(2,1)} async-done(((bf16[128,3,8,256]{0,3,1,2:T(8,128)(2,1)}), bf16[128,3,8,256]{0,3,1,2:T(8,128)(2,1)}, u32[]{:S(2)}, u32[]{:S(2)}) %all-to-all-start) | async-done | bytes 1572896 | tf_op jit(solution)/shard_map/all_to_all | solution.py:203
  204.9 3.6 copy.92
  208.5 3.7 reshape.381
  212.2 2.6 slice_bitcast_fusion.6
  215.6 21.5 %while.27 = (s32[]{:T(128)}, bf16[2,512,4,64]{1,3,2,0:T(8,128)(2,1)}, f32[2,4,512]{2,1,0:T(4,128)S(1)}, s32[2]{0:T(128)S(1)}, s32[1024]{0:T(1024)S(1)}, /*index=...) while((s32[]{:T(128)}, ...), condition=%wide.region_10.11_spmd, body=%wide.region_7.10_spmd.sunk | while | flops 563608064 | bytes 35469596 | solution.py:90
  217.5 2.6 fusion.126
  222.5 3.0 fusion.128
  228.3 2.6 fusion.126
  233.3 3.0 fusion.128
  243.5 4.2 all-to-all-start.1
  247.8 9.7 all-to-all-done.1
  257.5 4.9 fusion.81
  267.0 33.4 %all-gather.9.cloned.1.call-done = bf16[1024,2048]{1,0:T(8,128)(2,1)} async-done(((bf16[128,2048]{1,0:T(8,128)(2,1)}), bf16[1024,2048]{1,0:T(8,128)(2,1)}) %all-gather.9.cloned.1.call-update) | async-done | bytes 4194320 | tf_op jit(solution)/shard_map/all_gather | solution.py:145
  300.4 11.0 fusion.39
  311.4 28.1 %all-gather.11.cloned.1.call-done = bf16[1024,2048]{1,0:T(8,128)(2,1)} async-done(((bf16[128,2048]{1,0:T(8,128)(2,1)}), bf16[1024,2048]{1,0:T(8,128)(2,1)}) %all-gather.11.cloned.1.call-update) | async-done | bytes 4194320 | tf_op jit(solution)/shard_map/all_gather | solution.py:145
  339.5 8.3 fusion.45
  349.4 11.0 bitcast_convert_fusion
  360.5 6.4 convolution_convert_fusion.3
  366.9 45.0 %reduce-scatter.10.cloned.1.call-done = bf16[128,2048]{1,0:T(8,128)(2,1)} async-done(((bf16[1024,2048]{1,0:T(8,128)(2,1)}), bf16[128,2048]{1,0:T(8,128)(2,1)}) %reduce-scatter.10.cloned.1.call-update) | async-done | bytes 524304 | tf_op jit(solution)/shard_map/reduce_scatter | solution.py:149
  414.0 53.4 %reduce-scatter.8.cloned.1.call-done = bf16[128,2048]{1,0:T(8,128)(2,1)} async-done(((bf16[1024,2048]{1,0:T(8,128)(2,1)}), bf16[128,2048]{1,0:T(8,128)(2,1)}) %reduce-scatter.8.cloned.1.call-update) | async-done | bytes 524304 | tf_op jit(solution)/shard_map/reduce_scatter | solution.py:149
  469.7 7.1 convolution_convert_fusion.1
  476.9 6.3 convolution_convert_fusion.5
  484.0 3.5 all-to-all-start.2
  487.7 9.4 all-to-all-done.2
  501.1 32.1 %while.28 = (s32[]{:T(128)}, f32[1024,4,64]{0,2,1:T(8,128)S(1)}, f32[1024,4,64]{0,2,1:T(8,128)}, bf16[2,512,4,64]{1,3,2,0:T(8,128)(2,1)}, s32[2]{0:T(128)S(1)}, ...) while((s32[]{:T(128)}, f32[1024,4,64]{0,2,1:T(8,128)S(1)}, ...), condition=%wide.region_19.20_spmd.clone, body=%wide.region_17.19_spmd.clone.sunk | while | flops 1376647680 | bytes 87103920 | solution.py:125
  509.2 3.2 multiply_reduce_fusion.4
  522.6 2.6 fusion.141
  525.2 3.2 multiply_reduce_fusion.4
  538.0 2.9 copy.98
  541.0 29.3 %all_to_all.56 = bf16[1024,3,1,256]{3,1,2,0:T(4,128)(2,1)S(1)} all-to-all(bf16[1024,3,1,256]{3,1,2,0:T(4,128)(2,1)S(1)} %copy.98), channel_id=1, replica_groups=mesh['grp'=4,'seq'=8] {'seq'}, dimensions={0} | all-to-all | bytes 3145728 | tf_op jit(solution)/shard_map/all_to_all | solution.py:267
  578.7 12.0 convolution_convert_fusion
  590.7 10.8 convolution_convert_fusion.2
  603.2 8.9 convolution_convert_fusion.4
  612.1 134.8 %reduce-scatter.12.cloned.1.call-done = bf16[2048,3,256]{2,0,1:T(8,128)(2,1)} async-done(((bf16[2048,3,2048]{2,0,1:T(8,128)(2,1)}), bf16[2048,3,256]{2,0,1:T(8,128)(2,1)}) %reduce-scatter.12.cloned.1.call-update) | async-done | bytes 3145744 | tf_op jit(solution)/shard_map/reduce_scatter | solution.py:277
  746.9 14.6 %fusion.59 = (f32[2048]{0:T(1024)S(1)}, f32[128]{0:T(128)S(1)}, f32[128]{0:T(128)S(1)}, f32[2048]{0:T(1024)S(1)}, f32[128,2048]{1,0:T(8,128)}) fusion(bf16[128,2048]{1,0:T(8,128)(2,1)S(1)} %copy-done.6, f32[128]{0:T(128)S(1)} %copy-done.35, f32[128]{0:T(128)S(1)} %copy-done.33, f32[2048]{0:T(1024)S(1)} %bitcast.193, ...), kind=kOutput, calls=%fused_computation.93 | convolution fusion | flops 3225415680 | bytes 28338176 | tf_op jit(solution)/shard_map/tcf,dcf->td/dot_general | solution.py:273
  761.6 23.1 %all-reduce = (f32[2,2048]{1,0:T(2,128)S(1)}, f32[2,2048]{1,0:T(2,128)S(1)}) all-reduce(f32[2,2048]{1,0:T(2,128)S(1)} %pad_maximum_fusion.10, f32[2,2048]{1,0:T(2,128)S(1)} %pad_maximum_fusion.11), channel_id=1, replica_groups=mesh['grp'=4,'seq'=8] {'seq'}, use_global_device_ids=true, to_apply=%region_24.25 | all-reduce | flops 8192 | bytes 65536 | tf_op jit(solution)/shard_map/psum | solution.py:297
  784.7 20.2 %all-reduce.1 = (f32[2,2048]{1,0:T(2,128)}, f32[2,2048]{1,0:T(2,128)}) all-reduce(f32[2,2048]{1,0:T(2,128)S(1)} %get-tuple-element.211, f32[2,2048]{1,0:T(2,128)S(1)} %get-tuple-element.212), channel_id=1, replica_groups=mesh['grp'=4,'seq'=8] {'grp'}, use_global_device_ids=true, to_apply=%region_25.26 | all-reduce | flops 8192 | bytes 65536 | tf_op jit(solution)/shard_map/psum | solution.py:296
  808.3 11.3 psum.68
  820.3 405.0 %all-reduce.5.cloned.1.call-done = (bf16[2048,3,256]{2,0,1:T(8,128)(2,1)}, bf16[256,2048]{1,0:T(8,128)(2,1)}, bf16[2048,2,704]{0,2,1:T(8,128)(2,1)}, bf16[704,2048]{1,0:T(8,128)(2,1)}) async-done(((bf16[2048,3,256]{2,0,1:T(8,128)(2,1)}, bf16[256,2048]{1,0:T(8,128)(2,1)}, bf16[2048,2,704]{0,2,1:T(8,128)(2,1)}, bf16[704,2048]{1,0:T(8,128)(2,1)}), (bf16[2048,3,256]{2,0,1:T(8,128)(2,1)}, ...) | async-done | bytes 12845072 | tf_op jit(solution)/shard_map/psum | solution.py:290
  1225.3 2.9 convert_element_type.164
  1228.2 3.7 convert_element_type.161
  1232.0 3.3 convert_element_type.168
  1235.3 6.0 convert_element_type.166
  (233 shorter events, 77.3 us)
Async XLA Ops:
  7.2 332.3 %copy-start = (bf16[704,2048]{1,0:T(8,128)(2,1)S(1)}, bf16[704,2048]{1,0:T(8,128)(2,1)}, u32[]{:S(2)}) copy-start(bf16[704,2048]{1,0:T(8,128)(2,1)} %param.22) | copy-start | bytes 8650756
  7.2 1.6 copy-start.38
  7.2 2.3 copy-start.36
  7.2 12.8 %copy-start.5 = (bf16[128,2048]{1,0:T(8,128)(2,1)S(1)}, bf16[128,2048]{1,0:T(8,128)(2,1)}, u32[]{:S(2)}) copy-start(bf16[128,2048]{1,0:T(8,128)(2,1)} %param.15) | copy-start | bytes 1572868
  7.2 14.6 %copy-start.30 = (f32[2,2048]{1,0:T(2,128)S(1)}, f32[2,2048]{1,0:T(2,128)}, u32[]{:S(2)}) copy-start(f32[2,2048]{1,0:T(2,128)} %param.16) | copy-start | bytes 49156
  7.2 14.6 %copy-start.31 = (f32[2,2048]{1,0:T(2,128)S(1)}, f32[2,2048]{1,0:T(2,128)}, u32[]{:S(2)}) copy-start(f32[2,2048]{1,0:T(2,128)} %param.17) | copy-start | bytes 49156
  7.3 135.7 %all-gather.5.cloned.1.call-start = ((), (), s32[]{:S(2)}) async-start(), calls=%async_computation.9 | async-start | bytes 28311552 | tf_op jit(solution)/shard_map/all_gather | solution.py:187
  8.0 239.8 %all-gather.7.cloned.1.call-start = ((), (), s32[]{:S(2)}) async-start(), calls=%async_computation.10 | async-start | bytes 9437184 | tf_op jit(solution)/shard_map/all_gather | solution.py:189
  20.2 136.2 %copy-start.32 = (f32[128]{0:T(128)}, f32[128]{0:T(128)S(1)}, u32[]{:S(2)}) copy-start(f32[128]{0:T(128)S(1)} %broadcast_multiply_fusion.6) | copy-start | bytes 1540
  20.5 135.9 %copy-start.34 = (f32[128]{0:T(128)}, f32[128]{0:T(128)S(1)}, u32[]{:S(2)}) copy-start(f32[128]{0:T(128)S(1)} %add_rsqrt_fusion.1) | copy-start | bytes 1540
  21.9 141.2 %copy-start.25 = (f32[128,8]{0,1:T(8,128)}, f32[128,8]{0,1:T(8,128)S(1)}, u32[]{:S(2)}) copy-start(f32[128,8]{0,1:T(8,128)S(1)} %get-tuple-element.255) | copy-start | bytes 12292
  21.9 134.5 %copy-start.21 = (f32[1,2048]{1,0:T(1,128)}, f32[1,2048]{1,0:T(1,128)S(1)}, u32[]{:S(2)}) copy-start(f32[1,2048]{1,0:T(1,128)S(1)} %get-tuple-element.246) | copy-start | bytes 24580
  21.9 134.4 %copy-start.23 = (f32[1,2048]{1,0:T(1,128)}, f32[1,2048]{1,0:T(1,128)S(1)}, u32[]{:S(2)}) copy-start(f32[1,2048]{1,0:T(1,128)S(1)} %get-tuple-element.248) | copy-start | bytes 24580
  164.7 40.2 %all-to-all-start = ((bf16[128,3,8,256]{0,3,1,2:T(8,128)(2,1)}), bf16[128,3,8,256]{0,3,1,2:T(8,128)(2,1)}, u32[]{:S(2)}, u32[]{:S(2)}) async-start(bf16[128,3,8,256]{0,3,1,2:T(8,128)(2,1)} %copy.91), calls=%async_computation | async-start | bytes 3145728 | tf_op jit(solution)/shard_map/all_to_all | solution.py:203
  220.1 2.4 copy-start.7
  220.1 2.4 copy-start.16
  230.9 2.4 copy-start.7
  230.9 2.4 copy-start.16
  243.5 13.9 %all-to-all-start.1 = ((bf16[8,128,256]{1,2,0:T(8,128)(2,1)}), bf16[8,128,256]{1,2,0:T(8,128)(2,1)}, u32[]{:S(2)}, u32[]{:S(2)}) async-start(bf16[8,128,256]{1,2,0:T(8,128)(2,1)} %copy.94), calls=%async_computation.1 | async-start | bytes 1048576 | tf_op jit(solution)/shard_map/all_to_all | solution.py:213
  247.7 52.7 %all-gather.9.cloned.1.call-start = ((), (), s32[]{:S(2)}) async-start(), calls=%async_computation.11 | async-start | bytes 4718592 | tf_op jit(solution)/shard_map/all_gather | solution.py:145
  264.4 75.0 %all-gather.11.cloned.1.call-start = ((), (), s32[]{:S(2)}) async-start(), calls=%async_computation.13 | async-start | bytes 4718592 | tf_op jit(solution)/shard_map/all_gather | solution.py:145
  266.5 145.4 %reduce-scatter.10.cloned.1.call-start = ((), (), s32[]{:S(2)}) async-start(), calls=%async_computation.14 | async-start | bytes 4718592 | tf_op jit(solution)/shard_map/reduce_scatter | solution.py:149
  347.8 1.6 copy-start.40
  360.4 107.0 %reduce-scatter.8.cloned.1.call-start = ((), (), s32[]{:S(2)}) async-start(), calls=%async_computation.12 | async-start | bytes 4718592 | tf_op jit(solution)/shard_map/reduce_scatter | solution.py:149
  366.8 45.0 %copy-start.4 = (f32[128,2048]{1,0:T(8,128)S(1)}, f32[128,2048]{1,0:T(8,128)}, u32[]{:S(2)}) copy-start(f32[128,2048]{1,0:T(8,128)} %copy-done.3) | copy-start | bytes 3145732
  366.9 100.5 %copy-start.18 = (bf16[128,2048]{1,0:T(8,128)(2,1)S(1)}, bf16[128,2048]{1,0:T(8,128)(2,1)}, u32[]{:S(2)}) copy-start(bf16[128,2048]{1,0:T(8,128)(2,1)} %param.25) | copy-start | bytes 1572868
  366.9 245.2 %reduce-scatter.14.cloned.1.call-start = ((), (), s32[]{:S(2)}) async-start(), calls=%async_computation.16 | async-start | bytes 9437184 | tf_op jit(solution)/shard_map/reduce_scatter | solution.py:283
  469.7 7.1 copy-start.9
  483.1 18.0 %copy-start.2 = (bf16[1024,4,64]{0,2,1:T(8,128)(2,1)S(1)}, bf16[1024,4,64]{0,2,1:T(8,128)(2,1)}, u32[]{:S(2)}) copy-start(bf16[1024,4,64]{0,2,1:T(8,128)(2,1)} %get-tuple-element.492) | copy-start | bytes 1572868
  483.1 18.0 %copy-start.8 = (bf16[1024,4,64]{0,2,1:T(8,128)(2,1)S(1)}, bf16[1024,4,64]{0,2,1:T(8,128)(2,1)}, u32[]{:S(2)}) copy-start(bf16[1024,4,64]{0,2,1:T(8,128)(2,1)} %get-tuple-element.493) | copy-start | bytes 1572868
  484.0 13.2 %all-to-all-start.2 = ((bf16[128,8,256]{2,0,1:T(8,128)(2,1)}), bf16[128,8,256]{2,0,1:T(8,128)(2,1)S(1)}, u32[]{:S(2)}, u32[]{:S(2)}) async-start(bf16[128,8,256]{2,0,1:T(8,128)(2,1)} %bitcast.142), calls=%async_computation.4 | async-start | bytes 1048576 | tf_op jit(solution)/shard_map/all_to_all | solution.py:256
  487.5 259.4 %reduce-scatter.12.cloned.1.call-start = ((), (), s32[]{:S(2)}) async-start(), calls=%async_computation.15 | async-start | bytes 28311552 | tf_op jit(solution)/shard_map/reduce_scatter | solution.py:277
  509.2 3.2 copy-start.20
  512.3 2.4 copy-start.14
  525.2 3.2 copy-start.20
  528.4 2.4 copy-start.14
  575.6 2.1 copy-start.26
  575.6 2.1 copy-start.29
  590.7 216.7 %reduce-scatter.16.cloned.1.call-start = ((), (), s32[]{:S(2)}) async-start(), calls=%async_computation.17 | async-start | bytes 589824
  602.9 622.4 %all-reduce.5.cloned.1.call-start = ((), (), s32[]{:S(2)}) async-start(), calls=%async_computation.18 | async-start | bytes 25690112 | tf_op jit(solution)/shard_map/psum | solution.py:290
  746.9 14.7 %copy-start.28 = (f32[2048]{0:T(1024)S(1)}, f32[2048]{0:T(1024)}, u32[]{:S(2)}) copy-start(f32[2048]{0:T(1024)} %get-tuple-element.165) | copy-start | bytes 24580
  746.9 14.7 %copy-start.27 = (f32[2048]{0:T(1024)S(1)}, f32[2048]{0:T(1024)}, u32[]{:S(2)}) copy-start(f32[2048]{0:T(1024)} %get-tuple-element.170) | copy-start | bytes 24580
  746.9 58.0 %copy-start.10 = (f32[128,2048]{1,0:T(8,128)S(1)}, f32[128,2048]{1,0:T(8,128)}, u32[]{:S(2)}) copy-start(f32[128,2048]{1,0:T(8,128)} %copy-done.9) | copy-start | bytes 3145732
  1225.3 2.9 copy-start.12
  1225.3 10.0 slice-start
  1228.2 3.7 copy-start.13
  1228.2 7.1 slice-start.1
  1235.3 6.0 copy-start.1
  (16 other events, 17.8 us)
Sparse Core Ops, SparseCore 0:
  10.0 132.9 all-gather.4
  144.9 68.7 all-gather.6
  264.5 35.8 all-gather.8
  302.7 36.7 all-gather.10
  360.5 51.3 reduce-scatter.9
  416.0 51.2 reduce-scatter.7
  477.0 71.2 reduce-scatter.13
  590.8 156.0 reduce-scatter.11
  750.2 34.1 reduce-scatter.15
  788.3 436.9 all-reduce.4
